TPU v7x, 256 devices: a whole 4x4x8 slice. The times are simulated.
256 devices in a mesh: dp: 4 (over x), table: 64 (over y, z, core).
Axes of the slice: x: 4, y: 4, z: 8, core: 2. Of those that a mesh axis runs over, the one named last changes fastest.
Arguments:
- shard_of: int32 [2048, 200, 3], P(('dp', 'table')), may hold values from 0 to 63, all different within a row; in each aligned block of 1600 rows (0 to 1599, 1600 to 3199, ..., all dimensions but the last counted through in order) at most 152 rows name the same one
- offsets: int32 [2048, 200, 3], P(('dp', 'table')), may hold values from 0 to 2047
- table: bfloat16 [3, 131072, 256], P(None, 'table'), may hold values from -4 to 4
- weight_one: bfloat16 [768, 256], replicated, may hold values from -0.21875 to 0.21875
- gain_one: float32 [256], replicated, may hold values from 0.5 to 1.5
- weight_two: bfloat16 [768, 256], replicated, may hold values from -0.21875 to 0.21875
- gain_two: float32 [256], replicated, may hold values from 0.5 to 1.5
- grad_out: bfloat16 [2048, 200, 256], P(('dp', 'table')), may hold values from -6 to 6
Outputs:
- block_out: bfloat16 [2048, 200, 256], P(('dp', 'table'))
- grad_weight_one: float32 [768, 256], replicated
- grad_weight_two: float32 [768, 256], replicated
- grad_gain_one: float32 [256], replicated
- grad_gain_two: float32 [256], replicated
- table_grad: float32 [3, 131072, 256], P(None, 'table', 'dp')
Inputs may be any that keep to these rules, and one draw needn't show every extreme that they name: `shard_of`: the three lookups of one item go to three different shards; at most 152 lookups of the items of one device go to one shard, and exactly 152 for some shard of some device.
All inputs are finite; a program needn't handle non-finite values.
Results may differ from a plain program's by a relative error of at most 0.017.
Values may be sent and summed in bfloat16 or wider, within the bound.
A program may use at most 128 MiB of HBM per device.

v0:
```python
import math
import jax
import jax.numpy as jnp
from jax import lax
from jax.sharding import PartitionSpec as P

GELU_C = 0.7978845608028654
GELU_K = 0.044715


def shifted(values, spacing):
    return jnp.pad(values, ((0, 0), (spacing, 0), (0, 0)))[:, : values.shape[1], :]


def unshifted(values, spacing):
    return jnp.pad(values, ((0, 0), (0, spacing), (0, 0)))[:, spacing:, :]


def stack_taps(values, spacing):
    return jnp.concatenate(
        [values, shifted(values, spacing), shifted(values, 2 * spacing)], axis=-1
    )


def gelu_parts(inputs):
    inner = GELU_C * (inputs + GELU_K * inputs * inputs * inputs)
    tangent = jnp.tanh(inner)
    output = 0.5 * inputs * (1.0 + tangent)
    slope = 0.5 * (1.0 + tangent) + 0.5 * inputs * (1.0 - tangent * tangent) * GELU_C * (
        1.0 + 3.0 * GELU_K * inputs * inputs
    )
    return (output, slope)


def layer_forward(values, weight, gain, spacing):
    sessions, length, width = values.shape
    stacked = stack_taps(values, spacing).reshape(sessions * length, 3 * width)
    before_norm = jnp.dot(stacked, weight, preferred_element_type=jnp.float32)
    centred = before_norm - jnp.mean(before_norm, axis=-1, keepdims=True)
    inv_std = lax.rsqrt(jnp.mean(centred * centred, axis=-1, keepdims=True) + 1e-05)
    normal = centred * inv_std
    output, slope = gelu_parts(normal * gain)
    return (output, (stacked, normal, inv_std, slope))


def layer_backward(grad_output, weight, gain, saved, spacing, sessions, length):
    stacked, normal, inv_std, slope = saved
    width = weight.shape[1]
    grad_scaled = grad_output * slope
    grad_gain = jnp.sum(grad_scaled * normal, axis=0)
    grad_normal = grad_scaled * gain
    grad_before = inv_std * (
        grad_normal
        - jnp.mean(grad_normal, axis=-1, keepdims=True)
        - normal * jnp.mean(grad_normal * normal, axis=-1, keepdims=True)
    )
    grad_before = grad_before.astype(jnp.bfloat16)
    grad_weight = lax.dot_general(
        stacked, grad_before, (((0,), (0,)), ((), ())), preferred_element_type=jnp.float32
    )
    grad_taps = lax.dot_general(
        grad_before, weight, (((1,), (1,)), ((), ())), preferred_element_type=jnp.float32
    ).reshape(sessions, length, 3 * width)
    grad_input = (
        grad_taps[..., :width]
        + unshifted(grad_taps[..., width : 2 * width], spacing)
        + unshifted(grad_taps[..., 2 * width :], 2 * spacing)
    )
    return (grad_input, grad_weight, grad_gain)


def to_owners(grad_rows, slot_place, shards, slot_count, width):
    outgoing = (
        jnp.zeros((shards * slot_count, width), jnp.bfloat16)
        .at[slot_place]
        .set(grad_rows)
        .reshape(shards, slot_count, width)
    )
    return lax.all_to_all(outgoing, "table", split_axis=0, concat_axis=0, tiled=True)


def on_device(shard_of, offsets, table, weight_one, gain_one, weight_two, gain_two, grad_out):
    sessions, length, _ = shard_of.shape
    width = table.shape[2]
    rows_dev = table.shape[1]
    item_count = sessions * length
    shards = lax.axis_size("table")
    groups = lax.axis_size("dp")
    quarter = width // groups
    slot_count = 8 * ((6 * item_count + 8 * shards - 1) // (8 * shards))
    target = shard_of.reshape(-1)
    table_pick = jnp.tile(jnp.arange(3, dtype=jnp.int32), item_count)
    row_codes = table_pick * rows_dev + offsets.reshape(-1)
    onehot = (jnp.arange(shards, dtype=jnp.int32)[:, None] == target[None, :]).astype(jnp.int32)
    before = jnp.cumsum(onehot, axis=1) - onehot
    slot_rank = jnp.sum(before * onehot, axis=0)
    slot_place = target * slot_count + slot_rank
    requests = (
        jnp.full((shards * slot_count,), -1, jnp.int32)
        .at[slot_place]
        .set(row_codes)
        .reshape(shards, slot_count)
    )
    table_flat = table.reshape(3 * rows_dev, width)
    asked_rows = lax.all_to_all(requests, "table", split_axis=0, concat_axis=0, tiled=True)
    found_rows = jnp.take(table_flat, jnp.maximum(asked_rows, 0), axis=0)
    found_rows = jnp.where((asked_rows >= 0)[..., None], found_rows, jnp.zeros((), jnp.bfloat16))
    sent_back = lax.all_to_all(found_rows, "table", split_axis=0, concat_axis=0, tiled=True)
    picked = jnp.take(sent_back.reshape(shards * slot_count, width), slot_place, axis=0).reshape(
        item_count, 3, width
    )
    embedded = (
        jnp.sum(picked.astype(jnp.float32), axis=1)
        .astype(jnp.bfloat16)
        .reshape(sessions, length, width)
    )
    act_one, saved_one = layer_forward(embedded, weight_one, gain_one, 1)
    hidden = act_one.astype(jnp.bfloat16).reshape(sessions, length, width)
    act_two, saved_two = layer_forward(hidden, weight_two, gain_two, 2)
    block_out = (
        (embedded.reshape(item_count, width).astype(jnp.float32) + act_two)
        .astype(jnp.bfloat16)
        .reshape(sessions, length, width)
    )
    grad_top = grad_out.reshape(item_count, width).astype(jnp.float32)
    scale = 1.0 / math.sqrt(item_count * groups * shards)
    grad_hidden, second_weights, second_gains = layer_backward(
        grad_top, weight_two, gain_two, saved_two, 2, sessions, length
    )
    grad_inner, first_weights, first_gains = layer_backward(
        grad_hidden.reshape(item_count, width), weight_one, gain_one, saved_one, 1, sessions, length
    )
    grad_embed = (grad_top + grad_inner.reshape(item_count, width)).astype(jnp.bfloat16)
    repeated = jnp.repeat(grad_embed, 3, axis=0)
    arrived = to_owners(repeated, slot_place, shards, slot_count, width)
    dense_grad = (
        jnp.zeros((3 * rows_dev, width), jnp.float32)
        .at[jnp.maximum(asked_rows, 0).reshape(-1)]
        .add(arrived.reshape(-1, width).astype(jnp.float32))
    )
    table_grad = lax.psum_scatter(
        dense_grad.astype(jnp.bfloat16), "dp", scatter_dimension=1, tiled=True
    ).astype(jnp.float32)
    table_grad = table_grad.reshape(3, rows_dev, quarter)
    totals = lax.psum((first_weights, second_weights, first_gains, second_gains), ("dp", "table"))
    return (
        block_out,
        totals[0] * scale,
        totals[1] * scale,
        totals[2] * scale,
        totals[3] * scale,
        table_grad,
    )


def solution(mesh):
    placed = (
        P(("dp", "table"), None, None),
        P(("dp", "table"), None, None),
        P(None, "table", None),
        P(),
        P(),
        P(),
        P(),
        P(("dp", "table"), None, None),
    )
    return jax.shard_map(
        on_device,
        mesh=mesh,
        in_specs=placed,
        out_specs=(P(("dp", "table"), None, None), P(), P(), P(), P(), P(None, "table", "dp")),
        check_vma=False,
    )
```

profile of v0, /device:TPU:2, one launch (start us, length us, event | category | flops | bytes accessed | tf_op | source)
XLA Modules:
  0.0 678.1 jit_solution(2011394004684885150)
XLA Ops:
  8.9 2.0 copy.48
  10.9 0.9 iota_multiply_fusion
  11.9 1.2 copy.53
  13.1 1.7 mul.226
  14.8 1.2 copy.54
  16.0 1.6 reshape.223
  17.7 1.6 reshape.220
  19.3 1.6 mul.229
  21.0 1.1 pad.33
  22.1 2.4 reshape.221
  24.6 35.5 %reduce-window.6 = s32[64,38,128]{2,1,0:T(8,128)} reduce-window(s32[64,38,128]{2,1,0:T(8,128)} %reshape.221, s32[]{:T(128)} %constant.37.clone.1), window={size=1x1x128 pad=0_0x0_0x127_0}, to_apply=%region_0.0 | reduce-window | flops 39534592 | bytes 2490372 | tf_op jit(solution)/shard_map/reduce-window
  60.1 2.8 slice.72
  62.8 1.9 copy.59
  64.9 1.6 broadcast_add_fusion
  67.1 22.8 %scatter_custom_fusion = s32[9728]{0:T(1024)S(1)} fusion(s32[4800]{0:T(1024)S(1)} %fusion.30, s32[4800]{0:T(1024)S(1)} %add.145, s32[]{:T(128)} %constant.40.clone.1), kind=kCustom, calls=%fused_computation.82 | custom fusion | bytes 38916 | tf_op jit(solution)/shard_map/scatter | solution.py:101
  90.1 21.6 %all_to_all.19 = s32[64,1,152]{2,1,0:T(1,128)S(1)} all-to-all(s32[64,1,152]{2,1,0:T(1,128)S(1)} %all_to_all.12), channel_id=1, replica_groups=mesh['dp'=4,'table'=64] {'table'}, dimensions={0} | all-to-all | bytes 77824 | tf_op jit(solution)/shard_map/all_to_all | solution.py:105
  111.8 27.6 %gather_fusion = bf16[9728,256]{1,0:T(8,128)(2,1)} fusion(bf16[6144,256]{1,0:T(8,128)(2,1)S(1)} %bitcast.55, s32[10240]{0:T(1024)S(1)} %pad_clamp_fusion), kind=kCustom, calls=%fused_computation | custom fusion | bytes 10000384 | tf_op jit(solution)/shard_map/jit(_take)/gather | solution.py:106
  139.5 8.1 %select_select_fusion = bf16[64,152,256]{2,1,0:T(8,128)(2,1)} fusion(bf16[64,152,256]{2,1,0:T(8,128)(2,1)} %bitcast.61, pred[64,152]{1,0:T(8,128)(4,1)S(1)} %get-tuple-element.57, pred[64,152]{1,0:T(8,128)(4,1)S(1)} %get-tuple-element.56), kind=kLoop, calls=%fused_computation.7 | loop fusion | flops 4980736 | bytes 9980928 | tf_op jit(solution)/shard_map/jit(_where)/select_n | solution.py:107
  147.6 6.2 all-to-all-start.1
  155.3 110.9 %all-to-all-done.1 = bf16[64,152,256]{2,1,0:T(8,128)(2,1)} async-done(((bf16[64,152,256]{2,1,0:T(8,128)(2,1)}), bf16[64,152,256]{2,1,0:T(8,128)(2,1)}, u32[]{:S(2)}, u32[]{:S(2)}) %all-to-all-start.1) | async-done | bytes 4980768 | tf_op jit(solution)/shard_map/all_to_all | solution.py:108
  266.2 13.8 %gather_fusion.1 = bf16[4800,256]{1,0:T(8,128)(2,1)S(1)} fusion(bf16[9728,256]{1,0:T(8,128)(2,1)} %bitcast.6, s32[5120]{0:T(1024)S(1)} %pad_clamp_fusion.1), kind=kCustom, calls=%fused_computation.1 | custom fusion | bytes 4934400 | tf_op jit(solution)/shard_map/jit(_take)/gather | solution.py:109
  280.0 3.8 gather.12
  283.8 13.2 %select_reduce_fusion = bf16[1600,256]{1,0:T(8,128)(2,1)S(1)} fusion(bf16[1600,3,256]{2,1,0:T(4,128)(2,1)} %gather.12, pred[1600,3]{1,0:T(8,128)(4,1)S(1)} %copy.52), kind=kLoop, calls=%fused_computation.8 | loop fusion | flops 2048000 | bytes 3281600 | tf_op jit(solution)/shard_map/reduce_sum | solution.py:113
  298.0 0.9 fusion.37
  299.6 1.1 multiply_convert_fusion.2
  302.1 0.9 fusion.38
  304.1 1.5 convert_multiply_fusion
  305.7 1.0 multiply_reduce_fusion
  306.7 2.4 multiply_convert_fusion.1
  310.6 1.7 fusion.20
  312.3 1.0 multiply_reduce_fusion.1
  313.3 1.3 multiply_convert_fusion
  316.3 7.5 %broadcast_in_dim.70 = bf16[1600,3,256]{2,1,0:T(4,128)(2,1)} broadcast(bf16[1600,256]{1,0:T(8,128)(2,1)S(1)} %fusion.9), dimensions={0,2} | broadcast | bytes 3276800 | tf_op jit(solution)/shard_map/broadcast_in_dim | solution.py:134
  323.8 7.2 %reshape.269 = bf16[4800,256]{1,0:T(8,128)(2,1)} reshape(bf16[1600,3,256]{2,1,0:T(4,128)(2,1)} %broadcast_in_dim.70) | data formatting | bytes 4915200 | tf_op jit(solution)/shard_map/reshape | solution.py:134
  331.0 28.4 %scatter_custom_fusion.1 = bf16[9728,256]{1,0:T(8,128)(2,1)} fusion(s32[4800]{0:T(1024)S(1)} %fusion.30, bf16[4800,256]{1,0:T(8,128)(2,1)} %reshape.269, bf16[]{:T(256)} %constant.72.clone.1), kind=kCustom, calls=%fused_computation.10 | custom fusion | bytes 4981248 | tf_op jit(solution)/shard_map/scatter | solution.py:76
  359.5 6.4 all-to-all-start.2
  366.0 3.6 fusion.24
  369.6 1.8 fusion.26
  371.4 111.0 %all-to-all-done.2 = bf16[64,152,256]{2,1,0:T(8,128)(2,1)} async-done(((bf16[64,152,256]{2,1,0:T(8,128)(2,1)}), bf16[64,152,256]{2,1,0:T(8,128)(2,1)}, u32[]{:S(2)}, u32[]{:S(2)}) %all-to-all-start.2) | async-done | bytes 4980768 | tf_op jit(solution)/shard_map/all_to_all | solution.py:79
  482.4 64.7 %scatter_custom_fusion.2 = f32[6144,256]{1,0:T(8,128)} fusion(s32[9728]{0:T(1024)S(1)} %reshape.243, bf16[9728,256]{1,0:T(8,128)(2,1)} %bitcast.24, f32[]{:T(128)} %constant.73.clone.1), kind=kCustom, calls=%fused_computation.5 | custom fusion | flops 4980736 | bytes 11272196 | tf_op jit(solution)/shard_map/scatter-add | solution.py:139
  547.1 3.1 convert_element_type.64
  550.2 3.1 copy.60
  553.4 76.3 %all-reduce.9 = (f32[256]{0:T(256)S(1)}, f32[256]{0:T(256)S(1)}) all-reduce(f32[256]{0:T(256)S(1)} %get-tuple-element.38, f32[256]{0:T(256)S(1)} %get-tuple-element.36), channel_id=1, replica_groups=mesh['dp'=4,'table'=64] {'dp','table'}, use_global_device_ids=true, to_apply=%region_16.17 | all-reduce | flops 512 | bytes 4096 | tf_op jit(solution)/shard_map/psum | solution.py:145
  630.8 33.9 %all-reduce.13.cloned.1.call-done = (f32[768,256]{1,0:T(8,128)}, f32[768,256]{1,0:T(8,128)}) async-done(((f32[768,256]{1,0:T(8,128)}, f32[768,256]{1,0:T(8,128)}), (f32[768,256]{1,0:T(8,128)}, f32[768,256]{1,0:T(8,128)})) %all-reduce.13.cloned.1.call-update) | async-done | bytes 1572880 | tf_op jit(solution)/shard_map/psum | solution.py:145
  664.7 2.2 broadcast_multiply_fusion.1
  666.9 1.0 broadcast_multiply_fusion
  667.8 1.4 bitcast_convert_fusion
  669.2 1.2 copy.70
  (83 shorter events, 12.1 us)
Async XLA Ops:
  8.0 103.8 %copy-start = (bf16[3,2048,256]{2,1,0:T(8,128)(2,1)S(1)}, bf16[3,2048,256]{2,1,0:T(8,128)(2,1)}, u32[]{:S(2)}) copy-start(bf16[3,2048,256]{2,1,0:T(8,128)(2,1)} %param.10) | copy-start | bytes 9437188
  8.9 5.9 copy-start.17
  147.6 118.6 %all-to-all-start.1 = ((bf16[64,152,256]{2,1,0:T(8,128)(2,1)}), bf16[64,152,256]{2,1,0:T(8,128)(2,1)}, u32[]{:S(2)}, u32[]{:S(2)}) async-start(bf16[64,152,256]{2,1,0:T(8,128)(2,1)} %select_select_fusion), calls=%async_computation.1 | async-start | bytes 9961472 | tf_op jit(solution)/shard_map/all_to_all | solution.py:108
  297.0 1.0 copy-start.16
  297.4 1.6 copy-start.8
  297.4 1.6 copy-start.10
  299.0 0.7 copy-start.18
  300.8 2.2 copy-start.6
  300.8 1.3 copy-start.15
  301.2 1.8 copy-start.12
  301.2 1.8 copy-start.13
  303.0 1.1 copy-start.7
  303.0 1.1 copy-start.19
  309.1 0.9 copy-start.2
  314.6 0.9 copy-start.4
  359.5 6.5 copy-start.3
  359.5 122.9 %all-to-all-start.2 = ((bf16[64,152,256]{2,1,0:T(8,128)(2,1)}), bf16[64,152,256]{2,1,0:T(8,128)(2,1)}, u32[]{:S(2)}, u32[]{:S(2)}) async-start(bf16[64,152,256]{2,1,0:T(8,128)(2,1)} %bitcast.60), calls=%async_computation.2 | async-start | bytes 9961472 | tf_op jit(solution)/shard_map/all_to_all | solution.py:79
  365.9 3.7 copy-start.5
  365.9 298.8 %all-reduce.13.cloned.1.call-start = ((), (), s32[]{:S(2)}) async-start(), calls=%async_computation.5 | async-start | bytes 3145728 | tf_op jit(solution)/shard_map/psum | solution.py:145
  365.9 3.6 copy-start.9
  365.9 3.6 copy-start.11
  371.4 296.4 %reduce-scatter.4.cloned.1.call-start = ((), (), s32[]{:S(2)}) async-start(), calls=%async_computation.4 | async-start | bytes 3932160
  664.7 2.2 copy-start.14
  667.8 2.6 copy-start.1
Sparse Core Ops, SparseCore 0:
  372.8 291.8 all-reduce.12
Sparse Core Ops, SparseCore 1:
  553.5 37.5 reduce-scatter.3
where the time goes:
time: 690 us; the launch traced here: 678 us
  waiting for transfers between devices  256 us (37%)
  other arithmetic  146 us (21%)
  local copies, waits for them, and re-layouts  140 us (20%)
  blocking collectives  97.9 us (14%)
  between operations  16.2 us (2%)
  starting transfers between devices  12.6 us (2%)
  matrix products  8.91 us (1%)
    all_to_all x1, waiting for transfers between devices, to_owners(): lax.all_to_all(outgoing, 'table', split_axis=0, concat_axis=0, tiled=True)  111 us
    all_to_all x1, waiting for transfers between devices, on_device(): lax.all_to_all(found_rows, 'table', split_axis=0, concat_axis=0, tiled=True)  111 us
    psum x1, blocking collectives, on_device(): lax.psum((first_weights, second_weights, first_gains, second_gains), ('dp...  76.3 us
    scatter-add x1, other arithmetic, on_device(): dense_grad = jnp.zeros((3 * rows_dev, width), jnp.float32).at[jnp.maximum...  64.7 us
    another operation x3, other arithmetic  37.3 us
    psum x1, waiting for transfers between devices, on_device(): lax.psum((first_weights, second_weights, first_gains, second_gains), ('dp...  33.9 us
    scatter x1, local copies, waits for them, and re-layouts, to_owners(): outgoing = jnp.zeros((shards * slot_count, width), jnp.bfloat16).at[slot_...  28.4 us
    gather x1, local copies, waits for them, and re-layouts, on_device(): found_rows = jnp.take(table_flat, jnp.maximum(asked_rows, 0), axis=0)  27.6 us
  transfers between devices with their start and end apart: 4, of which 3 were waited for; matrix products, arithmetic and copies ran while one was open for 12% of the time, Pallas kernels for 0%

commit v1 on v0

--- a/solution.py
+++ b/solution.py
@@ -142,7 +142,9 @@
         dense_grad.astype(jnp.bfloat16), "dp", scatter_dimension=1, tiled=True
     ).astype(jnp.float32)
     table_grad = table_grad.reshape(3, rows_dev, quarter)
-    totals = lax.psum((first_weights, second_weights, first_gains, second_gains), ("dp", "table"))
+    totals = (first_weights, second_weights, first_gains, second_gains)
+    for mesh_axis in ("table", "dp"):
+        totals = lax.psum(totals, mesh_axis)
     return (
         block_out,
         totals[0] * scale,

time: 690 us -> 819 us (1.19)
  waiting for transfers between devices: 256 us -> 328 us
  blocking collectives: 97.9 us -> 157 us
    psum x1 -> x2, waiting for transfers between devices: 33.9 us -> 217 us  [on_device(): totals = lax.psum(totals, mesh_axis)]
    all_to_all x1, waiting for transfers between devices: 111 us -> 0.01 us  [to_owners(): lax.all_to_all(outgoing, 'table', split_axis=0, concat_axis=0, tiled=True)]
    psum x1 -> x2, blocking collectives: 76.3 us -> 135 us  [on_device(): totals = lax.psum(totals, mesh_axis)]
  transfers between devices with their start and end apart: 4 -> 5, of which waited for: 3 -> 2; matrix products, arithmetic and copies ran while one was open for 12% -> 10% of each run, Pallas kernels for 0% -> 0%
where the time goes in v1:
time: 819 us; the launch traced here: 807 us
  waiting for transfers between devices  328 us (40%)
  blocking collectives  157 us (19%)
  other arithmetic  146 us (18%)
  local copies, waits for them, and re-layouts  140 us (17%)
  between operations  14.5 us (2%)
  starting transfers between devices  12.7 us (2%)
  matrix products  8.91 us (1%)
    psum x2, waiting for transfers between devices, on_device(): totals = lax.psum(totals, mesh_axis)  217 us
    psum x2, blocking collectives, on_device(): totals = lax.psum(totals, mesh_axis)  135 us
    all_to_all x1, waiting for transfers between devices, on_device(): lax.all_to_all(found_rows, 'table', split_axis=0, concat_axis=0, tiled=True)  111 us
    scatter-add x1, other arithmetic, on_device(): dense_grad = jnp.zeros((3 * rows_dev, width), jnp.float32).at[jnp.maximum...  64.8 us
    another operation x3, other arithmetic  37.3 us
    scatter x1, local copies, waits for them, and re-layouts, to_owners(): outgoing = jnp.zeros((shards * slot_count, width), jnp.bfloat16).at[slot_...  28.3 us
    gather x1, local copies, waits for them, and re-layouts, on_device(): found_rows = jnp.take(table_flat, jnp.maximum(asked_rows, 0), axis=0)  27.6 us
    scatter x1, local copies, waits for them, and re-layouts, on_device(): requests = jnp.full((shards * slot_count,), -1, jnp.int32).at[slot_place]...  22.8 us
  transfers between devices with their start and end apart: 5, of which 2 were waited for; matrix products, arithmetic and copies ran while one was open for 10% of the time, Pallas kernels for 0%

profile of v1, /device:TPU:2, one launch (start us, length us, event | category | flops | bytes accessed | tf_op | source)
XLA Modules:
  0.0 807.3 jit_solution(11630807067674048858)
XLA Ops:
  8.1 2.0 copy.48
  10.1 0.9 iota_multiply_fusion
  11.0 1.2 copy.53
  12.2 1.7 mul.226
  14.0 1.2 copy.54
  15.2 1.6 reshape.223
  16.8 1.6 reshape.220
  18.5 1.6 mul.229
  20.2 1.1 pad.33
  21.3 2.4 reshape.221
  23.7 35.5 %reduce-window.6 = s32[64,38,128]{2,1,0:T(8,128)} reduce-window(s32[64,38,128]{2,1,0:T(8,128)} %reshape.221, s32[]{:T(128)} %constant.37.clone.1), window={size=1x1x128 pad=0_0x0_0x127_0}, to_apply=%region_0.0 | reduce-window | flops 39534592 | bytes 2490372 | tf_op jit(solution)/shard_map/reduce-window
  59.2 2.8 slice.72
  62.0 1.9 copy.59
  64.1 1.6 broadcast_add_fusion
  66.2 22.8 %scatter_custom_fusion = s32[9728]{0:T(1024)S(1)} fusion(s32[4800]{0:T(1024)S(1)} %fusion.30, s32[4800]{0:T(1024)S(1)} %add.153, s32[]{:T(128)} %constant.40.clone.1), kind=kCustom, calls=%fused_computation.82 | custom fusion | bytes 38916 | tf_op jit(solution)/shard_map/scatter | solution.py:101
  89.3 21.6 %all_to_all.19 = s32[64,1,152]{2,1,0:T(1,128)S(1)} all-to-all(s32[64,1,152]{2,1,0:T(1,128)S(1)} %all_to_all.12), channel_id=1, replica_groups=mesh['dp'=4,'table'=64] {'table'}, dimensions={0} | all-to-all | bytes 77824 | tf_op jit(solution)/shard_map/all_to_all | solution.py:105
  111.0 27.6 %gather_fusion = bf16[9728,256]{1,0:T(8,128)(2,1)} fusion(bf16[6144,256]{1,0:T(8,128)(2,1)S(1)} %bitcast.55, s32[10240]{0:T(1024)S(1)} %pad_clamp_fusion), kind=kCustom, calls=%fused_computation | custom fusion | bytes 10000384 | tf_op jit(solution)/shard_map/jit(_take)/gather | solution.py:106
  138.7 8.1 %select_select_fusion = bf16[64,152,256]{2,1,0:T(8,128)(2,1)} fusion(bf16[64,152,256]{2,1,0:T(8,128)(2,1)} %bitcast.61, pred[64,152]{1,0:T(8,128)(4,1)S(1)} %get-tuple-element.61, pred[64,152]{1,0:T(8,128)(4,1)S(1)} %get-tuple-element.60), kind=kLoop, calls=%fused_computation.7 | loop fusion | flops 4980736 | bytes 9980928 | tf_op jit(solution)/shard_map/jit(_where)/select_n | solution.py:107
  146.8 6.2 all-to-all-start.1
  154.5 110.9 %all-to-all-done.1 = bf16[64,152,256]{2,1,0:T(8,128)(2,1)} async-done(((bf16[64,152,256]{2,1,0:T(8,128)(2,1)}), bf16[64,152,256]{2,1,0:T(8,128)(2,1)}, u32[]{:S(2)}, u32[]{:S(2)}) %all-to-all-start.1) | async-done | bytes 4980768 | tf_op jit(solution)/shard_map/all_to_all | solution.py:108
  265.4 13.8 %gather_fusion.1 = bf16[4800,256]{1,0:T(8,128)(2,1)S(1)} fusion(bf16[9728,256]{1,0:T(8,128)(2,1)} %bitcast.6, s32[5120]{0:T(1024)S(1)} %pad_clamp_fusion.1), kind=kCustom, calls=%fused_computation.1 | custom fusion | bytes 4934400 | tf_op jit(solution)/shard_map/jit(_take)/gather | solution.py:109
  279.2 3.8 gather.12
  283.0 13.2 %select_reduce_fusion = bf16[1600,256]{1,0:T(8,128)(2,1)S(1)} fusion(bf16[1600,3,256]{2,1,0:T(4,128)(2,1)} %gather.12, pred[1600,3]{1,0:T(8,128)(4,1)S(1)} %copy.52), kind=kLoop, calls=%fused_computation.8 | loop fusion | flops 2048000 | bytes 3281600 | tf_op jit(solution)/shard_map/reduce_sum | solution.py:113
  297.2 0.9 fusion.37
  298.8 1.1 multiply_convert_fusion.2
  301.2 0.9 fusion.38
  303.3 1.5 convert_multiply_fusion
  304.8 1.0 multiply_reduce_fusion
  305.8 2.4 multiply_convert_fusion.1
  309.8 1.7 fusion.20
  311.5 1.0 multiply_reduce_fusion.1
  312.5 1.3 multiply_convert_fusion
  315.5 7.5 broadcast_in_dim.70
  323.0 7.2 reshape.269
  330.2 28.3 %scatter_custom_fusion.1 = bf16[9728,256]{1,0:T(8,128)(2,1)} fusion(s32[4800]{0:T(1024)S(1)} %fusion.30, bf16[4800,256]{1,0:T(8,128)(2,1)} %reshape.269, bf16[]{:T(256)} %constant.72.clone.1), kind=kCustom, calls=%fused_computation.10 | custom fusion | bytes 4981248 | tf_op jit(solution)/shard_map/scatter | solution.py:76
  358.5 6.4 all-to-all-start.2
  365.0 3.6 fusion.24
  368.6 1.8 fusion.26
  370.5 216.7 %all-reduce.16.cloned.1.call-done = (f32[768,256]{1,0:T(8,128)}, f32[768,256]{1,0:T(8,128)}) async-done(((f32[768,256]{1,0:T(8,128)}, f32[768,256]{1,0:T(8,128)}), (f32[768,256]{1,0:T(8,128)}, f32[768,256]{1,0:T(8,128)})) %all-reduce.16.cloned.1.call-update) | async-done | bytes 1572880 | tf_op jit(solution)/shard_map/psum | solution.py:147
  587.2 64.8 %scatter_custom_fusion.2 = f32[6144,256]{1,0:T(8,128)} fusion(s32[9728]{0:T(1024)S(1)} %reshape.243, bf16[9728,256]{1,0:T(8,128)(2,1)} %bitcast.24, f32[]{:T(128)} %constant.73.clone.1), kind=kCustom, calls=%fused_computation.5 | custom fusion | flops 4980736 | bytes 11272196 | tf_op jit(solution)/shard_map/scatter-add | solution.py:139
  652.0 3.1 convert_element_type.64
  655.1 3.1 copy.60
  658.2 127.0 %all-reduce.9 = (f32[256]{0:T(256)S(1)}, f32[256]{0:T(256)S(1)}) all-reduce(f32[256]{0:T(256)S(1)} %get-tuple-element.38, f32[256]{0:T(256)S(1)} %get-tuple-element.36), channel_id=1, replica_groups=mesh['dp'=4,'table'=64] {'table'}, use_global_device_ids=true, to_apply=%region_18.19 | all-reduce | flops 512 | bytes 4096 | tf_op jit(solution)/shard_map/psum | solution.py:147
  785.2 8.4 %all-reduce.11 = (f32[256]{0:T(256)S(1)}, f32[256]{0:T(256)S(1)}) all-reduce(f32[256]{0:T(256)S(1)} %get-tuple-element.42, f32[256]{0:T(256)S(1)} %get-tuple-element.43), channel_id=1, replica_groups=mesh['dp'=4,'table'=64] {'dp'}, use_global_device_ids=true, to_apply=%region_19.20 | all-reduce | flops 512 | bytes 4096 | tf_op jit(solution)/shard_map/psum | solution.py:147
  794.8 2.2 broadcast_multiply_fusion.1
  797.0 1.0 broadcast_multiply_fusion
  797.9 1.4 bitcast_convert_fusion
  799.3 1.2 copy.70
  (87 shorter events, 12.2 us)
Async XLA Ops:
  7.2 103.8 %copy-start = (bf16[3,2048,256]{2,1,0:T(8,128)(2,1)S(1)}, bf16[3,2048,256]{2,1,0:T(8,128)(2,1)}, u32[]{:S(2)}) copy-start(bf16[3,2048,256]{2,1,0:T(8,128)(2,1)} %param.10) | copy-start | bytes 9437188
  8.1 5.9 copy-start.17
  146.8 118.6 %all-to-all-start.1 = ((bf16[64,152,256]{2,1,0:T(8,128)(2,1)}), bf16[64,152,256]{2,1,0:T(8,128)(2,1)}, u32[]{:S(2)}, u32[]{:S(2)}) async-start(bf16[64,152,256]{2,1,0:T(8,128)(2,1)} %select_select_fusion), calls=%async_computation.1 | async-start | bytes 9961472 | tf_op jit(solution)/shard_map/all_to_all | solution.py:108
  296.2 1.0 copy-start.16
  296.6 1.6 copy-start.8
  296.6 1.6 copy-start.10
  298.1 0.7 copy-start.18
  299.9 2.2 copy-start.6
  300.0 1.3 copy-start.15
  300.3 1.8 copy-start.12
  300.3 1.8 copy-start.13
  302.2 1.1 copy-start.7
  302.2 1.1 copy-start.19
  308.2 0.9 copy-start.2
  313.8 0.9 copy-start.4
  358.5 6.5 copy-start.3
  358.5 228.7 %all-to-all-start.2 = ((bf16[64,152,256]{2,1,0:T(8,128)(2,1)}), bf16[64,152,256]{2,1,0:T(8,128)(2,1)}, u32[]{:S(2)}, u32[]{:S(2)}) async-start(bf16[64,152,256]{2,1,0:T(8,128)(2,1)} %bitcast.60), calls=%async_computation.2 | async-start | bytes 9961472 | tf_op jit(solution)/shard_map/all_to_all | solution.py:79
  364.9 3.7 copy-start.5
  364.9 222.2 %all-reduce.16.cloned.1.call-start = ((), (), s32[]{:S(2)}) async-start(), calls=%async_computation.5 | async-start | bytes 3145728 | tf_op jit(solution)/shard_map/psum | solution.py:147
  365.0 3.6 copy-start.9
  365.0 3.6 copy-start.11
  370.5 424.4 %all-reduce.18.cloned.1.call-start = ((), (), s32[]{:S(2)}) async-start(), calls=%async_computation.6 | async-start | bytes 3145728 | tf_op jit(solution)/shard_map/psum | solution.py:147
  587.2 210.7 %reduce-scatter.4.cloned.1.call-start = ((), (), s32[]{:S(2)}) async-start(), calls=%async_computation.4 | async-start | bytes 3932160
  794.8 2.2 copy-start.14
  797.9 2.6 copy-start.1
Sparse Core Ops, SparseCore 0:
  370.6 216.5 all-reduce.15
  589.5 53.3 all-reduce.17
  658.3 36.4 reduce-scatter.3
